TPU v7x, 128 devices: a whole 4x4x4 slice. The times are simulated.
128 devices in a mesh: row: 8 (over y_lo, x), col: 16 (over z, y_hi, core).
Axes of the slice: x: 4, y: 4 (y_hi: 2, y_lo: 2; y = y_hi * 2 + y_lo), z: 4, core: 2. Of those that a mesh axis runs over, the one named last changes fastest.
Arguments:
- points: bfloat16 [64, 65536], P(None, ('row', 'col')), may hold values from -6 to 6
- solution: float32 [16, 65536], P(None, ('row', 'col')), may hold values from -6 to 6
- residual: float32 [16, 65536], P(None, ('row', 'col')), may hold values from -6 to 6
- direction: float32 [16, 65536], P(None, ('row', 'col')), may hold values from -6 to 6
Outputs:
- solution_next: float32 [16, 65536], P(None, ('row', 'col'))
- residual_next: float32 [16, 65536], P(None, ('row', 'col'))
- direction_next: float32 [16, 65536], P(None, ('row', 'col'))
All inputs are finite; a program needn't handle non-finite values.
Results may differ from a plain program's by a relative error of at most 0.0042.
Values may be sent and summed in bfloat16 or wider, within the bound.
A program may use at most 64 MiB of HBM per device.

v0:
```python
import jax
import jax.numpy as jnp
import numpy as np
from jax import lax
from jax.sharding import PartitionSpec as P

F = 64
TILE = 2048


def pair_table(tile_count, device_count):
    pairs = [(i, j) for i in range(tile_count) for j in range(i, tile_count)]
    slot_count = (len(pairs) + device_count - 1) // device_count
    table = np.full((device_count, slot_count, 2), tile_count, np.int32)
    for position, pair in enumerate(pairs):
        table[position % device_count, position // device_count, 0] = pair[0]
        table[position % device_count, position // device_count, 1] = pair[1]
    return table


def add_columns(accumulated, column_start, piece):
    current = lax.dynamic_slice_in_dim(accumulated, column_start, piece.shape[1], 1)
    return lax.dynamic_update_slice_in_dim(accumulated, current + piece, column_start, 1)


def triangle_terms(everyone, sq_norms, all_directions, my_pairs):
    total_points = everyone.shape[1]
    tile_count = total_points // TILE
    block_rows = min(512, TILE)

    def one_pair(slot_index, accumulated):
        row_tile = my_pairs[slot_index, 0]
        col_tile = my_pairs[slot_index, 1]
        slot_live = row_tile < tile_count
        weight = slot_live.astype(jnp.float32)
        mirror = weight * (row_tile != col_tile).astype(jnp.float32)
        row_base = (jnp.minimum(row_tile, tile_count - 1) * TILE).astype(jnp.int32)
        col_start = (jnp.minimum(col_tile, tile_count - 1) * TILE).astype(jnp.int32)
        col_points = lax.dynamic_slice_in_dim(everyone, col_start, TILE, 1)
        col_norms = lax.dynamic_slice_in_dim(sq_norms, col_start, TILE, 0)
        col_vectors = lax.dynamic_slice_in_dim(all_directions, col_start, TILE, 1)
        mirrored = jnp.zeros((all_directions.shape[0], TILE), jnp.float32)
        for piece_index in range(TILE // block_rows):
            row_start = row_base + piece_index * block_rows
            row_points = lax.dynamic_slice_in_dim(everyone, row_start, block_rows, 1)
            row_norms = lax.dynamic_slice_in_dim(sq_norms, row_start, block_rows, 0)
            row_vectors = lax.dynamic_slice_in_dim(all_directions, row_start, block_rows, 1)
            cross_terms = lax.dot_general(
                row_points, col_points, (((0,), (0,)), ((), ())), preferred_element_type=jnp.float32
            )
            dist = row_norms[:, None] + col_norms[None, :] - 2.0 * cross_terms
            kernel = jnp.exp(-(2.0 / F) * dist).astype(jnp.bfloat16)
            row_terms = lax.dot_general(
                col_vectors, kernel, (((1,), (1,)), ((), ())), preferred_element_type=jnp.float32
            )
            accumulated = add_columns(accumulated, row_start, weight * row_terms)
            mirrored = mirrored + jnp.dot(row_vectors, kernel, preferred_element_type=jnp.float32)
        return add_columns(accumulated, col_start, mirror * mirrored)

    return lax.fori_loop(
        0,
        my_pairs.shape[0],
        one_pair,
        jnp.zeros((all_directions.shape[0], total_points), jnp.float32),
    )


def on_device(points, solution, residual, direction):
    local_width = points.shape[1]
    everyone = lax.all_gather(points, ("row", "col"), axis=1, tiled=True)
    total_points = everyone.shape[1]
    tile_count = total_points // TILE
    sq_norms = jnp.sum(jnp.square(everyone.astype(jnp.float32)), axis=0)
    all_directions = lax.all_gather(
        direction.astype(jnp.bfloat16), ("row", "col"), axis=1, tiled=True
    )
    table = jnp.asarray(pair_table(tile_count, lax.axis_size(("row", "col"))))
    my_pairs = table[lax.axis_index(("row", "col"))]
    accumulated = triangle_terms(everyone, sq_norms, all_directions, my_pairs)
    summed = lax.psum(accumulated, ("row", "col"))
    own_start = lax.axis_index(("row", "col")) * local_width
    own_rows = lax.dynamic_slice_in_dim(summed, own_start, local_width, 1)
    image_rows = 1.0 * direction + own_rows
    old_norm = lax.psum(jnp.sum(residual * residual, axis=1), ("row", "col"))
    curvature = lax.psum(jnp.sum(direction * image_rows, axis=1), ("row", "col"))
    step_size = old_norm / curvature
    residual_next = residual - step_size[:, None] * image_rows
    new_norm = lax.psum(jnp.sum(residual_next * residual_next, axis=1), ("row", "col"))
    solution_next = solution + step_size[:, None] * direction
    direction_next = residual_next + (new_norm / old_norm)[:, None] * direction
    return (solution_next, residual_next, direction_next)


def solution(mesh):
    placed = (
        P(None, ("row", "col")),
        P(None, ("row", "col")),
        P(None, ("row", "col")),
        P(None, ("row", "col")),
    )
    return jax.shard_map(
        on_device,
        mesh=mesh,
        in_specs=placed,
        out_specs=(P(None, ("row", "col")), P(None, ("row", "col")), P(None, ("row", "col"))),
        check_vma=False,
    )
```

profile of v0, /device:TPU:1, one launch (start us, length us, event | category | flops | bytes accessed | tf_op | source)
XLA Modules:
  0.0 835.4 jit_solution(7481728378052199383)
XLA Ops:
  7.9 1.4 convert_element_type.62
  10.1 204.3 %all-gather.5.cloned.1.call-done = bf16[64,65536]{1,0:T(8,128)(2,1)} async-done(((bf16[64,512]{1,0:T(8,128)(2,1)}), bf16[64,65536]{1,0:T(8,128)(2,1)}) %all-gather.5.cloned.1.call-update) | async-done | bytes 8388624 | tf_op jit(solution)/shard_map/all_gather | solution.py:70
  214.4 5.5 multiply_reduce_fusion
  219.9 191.2 %all-gather.3.cloned.1.call-done = bf16[16,65536]{1,0:T(8,128)(2,1)} async-done(((bf16[16,512]{1,0:T(8,128)(2,1)}), bf16[16,65536]{1,0:T(8,128)(2,1)}) %all-gather.3.cloned.1.call-update) | async-done | bytes 2097168 | tf_op jit(solution)/shard_map/all_gather | solution.py:74
  411.0 2.2 broadcast_in_dim.24
  413.3 131.7 %while.15 = (s32[]{:T(128)}, f32[16,65536]{1,0:T(8,128)}, s32[5,2]{0,1:T(2,128)S(1)}, bf16[16,65536]{1,0:T(8,128)(2,1)}, f32[65536]{0:T(1024)S(1)}, /*index=5*/b...) while((s32[]{:T(128)}, f32[16,65536]{1,0:T(8,128)}, ...), condition=%wide.region_4.0_spmd, body=%wide.region_3.0_spmd.sunk | while | flops 826507264 | bytes 28191316 | solution.py:60
  417.3 2.1 exponential_convert_fusion.8
  420.5 2.1 fusion.105
  422.6 2.1 exponential_convert_fusion.9
  424.8 1.1 convolution_add_fusion.5
  425.9 2.1 fusion.106
  428.0 2.1 exponential_convert_fusion.10
  430.1 1.1 convolution_add_fusion.6
  431.2 2.1 fusion.107
  433.4 2.1 exponential_convert_fusion.11
  435.5 2.1 fusion.108
  437.6 2.0 fusion.110
  443.6 2.1 exponential_convert_fusion.8
  446.8 2.1 fusion.105
  448.9 2.1 exponential_convert_fusion.9
  451.1 1.1 convolution_add_fusion.5
  452.2 2.1 fusion.106
  454.3 2.1 exponential_convert_fusion.10
  456.4 1.1 convolution_add_fusion.6
  457.6 2.1 fusion.107
  459.7 2.1 exponential_convert_fusion.11
  461.8 2.1 fusion.108
  463.9 2.0 fusion.110
  469.9 2.1 exponential_convert_fusion.8
  473.1 2.1 fusion.105
  475.2 2.1 exponential_convert_fusion.9
  477.4 1.1 convolution_add_fusion.5
  478.5 2.1 fusion.106
  480.6 2.1 exponential_convert_fusion.10
  482.8 1.1 convolution_add_fusion.6
  483.9 2.1 fusion.107
  486.0 2.1 exponential_convert_fusion.11
  488.1 2.1 fusion.108
  490.3 2.0 fusion.110
  496.2 2.1 exponential_convert_fusion.8
  499.4 2.1 fusion.105
  501.6 2.1 exponential_convert_fusion.9
  503.7 1.1 convolution_add_fusion.5
  504.8 2.1 fusion.106
  506.9 2.1 exponential_convert_fusion.10
  509.1 1.1 convolution_add_fusion.6
  510.2 2.1 fusion.107
  512.3 2.1 exponential_convert_fusion.11
  514.4 2.1 fusion.108
  516.5 2.0 fusion.110
  522.4 2.2 exponential_convert_fusion.8
  525.7 2.1 fusion.105
  527.9 2.2 exponential_convert_fusion.9
  530.0 1.1 convolution_add_fusion.5
  531.2 2.1 fusion.106
  533.3 2.2 exponential_convert_fusion.10
  536.6 2.1 fusion.107
  538.7 2.2 exponential_convert_fusion.11
  540.9 2.1 fusion.108
  543.0 2.0 fusion.110
  545.8 152.4 %all-reduce.3.cloned.1.call-done = f32[16,65536]{1,0:T(8,128)} async-done(((f32[16,65536]{1,0:T(8,128)}), f32[16,65536]{1,0:T(8,128)}) %all-reduce.3.cloned.1.call-update) | async-done | bytes 4194320 | tf_op jit(solution)/shard_map/psum | solution.py:80
  699.1 64.0 %all-reduce = (f32[16]{0:T(128)S(1)}, f32[16]{0:T(128)S(1)}) all-reduce(f32[16]{0:T(128)S(1)} %multiply_reduce_fusion.3, f32[16]{0:T(128)S(1)} %multiply_reduce_fusion.2), channel_id=1, replica_groups=mesh['row'=8,'col'=16] {'row','col'}, use_global_device_ids=true, to_apply=%region_1.0 | all-reduce | flops 32 | bytes 256 | tf_op jit(solution)/shard_map/psum | solution.py:84
  763.1 1.6 multiply_reduce_fusion.1
  764.6 63.5 %psum.31 = f32[16]{0:T(128)S(1)} all-reduce(f32[16]{0:T(128)S(1)} %get-tuple-element.174), channel_id=1, replica_groups=mesh['row'=8,'col'=16] {'row','col'}, use_global_device_ids=true, to_apply=%region_9.0 | all-reduce | flops 16 | bytes 128 | tf_op jit(solution)/shard_map/psum | solution.py:88
  (41 shorter events, 14.1 us)
Async XLA Ops:
  7.2 207.2 %all-gather.5.cloned.1.call-start = ((), (), s32[]{:S(2)}) async-start(), calls=%async_computation.1 | async-start | bytes 8454144 | tf_op jit(solution)/shard_map/all_gather | solution.py:70
  7.9 403.1 %all-gather.3.cloned.1.call-start = ((), (), s32[]{:S(2)}) async-start(), calls=%async_computation | async-start | bytes 2113536 | tf_op jit(solution)/shard_map/all_gather | solution.py:74
  9.3 688.9 %all-reduce.3.cloned.1.call-start = ((), (), s32[]{:S(2)}) async-start(), calls=%async_computation.2 | async-start | bytes 8388608 | tf_op jit(solution)/shard_map/psum | solution.py:80
  545.0 0.8 copy-start.2
  545.0 153.2 %copy-start = (f32[16,512]{1,0:T(8,128)S(1)}, f32[16,512]{1,0:T(8,128)}, u32[]{:S(2)}) copy-start(f32[16,512]{1,0:T(8,128)} %param.10) | copy-start | bytes 98308
  545.0 218.1 %copy-start.3 = (f32[16,512]{1,0:T(8,128)S(1)}, f32[16,512]{1,0:T(8,128)}, u32[]{:S(2)}) copy-start(f32[16,512]{1,0:T(8,128)} %param.8) | copy-start | bytes 98308
  764.6 64.2 %copy-start.1 = (f32[16,512]{1,0:T(8,128)}, f32[16,512]{1,0:T(8,128)S(1)}, u32[]{:S(2)}) copy-start(f32[16,512]{1,0:T(8,128)S(1)} %get-tuple-element.175) | copy-start | bytes 98308
Sparse Core Ops, SparseCore 0:
  9.7 204.6 all-gather.4
  216.7 194.2 all-gather.2
  545.1 153.0 all-reduce.2
where the time goes:
time: 838 us; the launch traced here: 835 us
  waiting for transfers between devices  549 us (66%)
  blocking collectives  128 us (15%)
  matrix products  112 us (13%)
  loops' own time  16.6 us (2%)
  between operations  13.8 us (2%)
  other arithmetic  10.1 us (1%)
    all_gather x1, waiting for transfers between devices, on_device(): everyone = lax.all_gather(points, ('row', 'col'), axis=1, tiled=True)  204 us
    all_gather x1, waiting for transfers between devices, on_device(): lax.all_gather(direction.astype(jnp.bfloat16), ('row', 'col'), axis=1, ti...  191 us
    psum x1, waiting for transfers between devices, on_device(): summed = lax.psum(accumulated, ('row', 'col'))  152 us
    psum x1, blocking collectives, on_device(): old_norm = lax.psum(jnp.sum(residual * residual, axis=1), ('row', 'col'))  64 us
    psum x1, blocking collectives, on_device(): lax.psum(jnp.sum(residual_next * residual_next, axis=1), ('row', 'col'))  63.5 us
    dot_general x20, matrix products, one_pair(): lax.dot_general(row_points, col_points, (((0,), (0,)), ((), ())), preferr...  42.8 us
    dot_general x20, matrix products, one_pair(): lax.dot_general(col_vectors, kernel, (((1,), (1,)), ((), ())), preferred_...  42.4 us
    dot_general x20, matrix products, one_pair(): jnp.dot(row_vectors, kernel, preferred_element_type=jnp.float32)  26.5 us
  transfers between devices with their start and end apart: 3, of which 3 were waited for; matrix products, arithmetic and copies ran while one was open for 1% of the time, Pallas kernels for 0%

commit v1 on v0

v1 whole, which is shorter than its diff:
```python
import math

import jax
import jax.numpy as jnp
from jax import lax
from jax.experimental import pallas as pl
from jax.experimental.pallas import tpu as pltpu
from jax.sharding import PartitionSpec as P

OWN = ((0, 0), (0, 1), (1, 0), (1, 1), (3, 0), (3, 1), (2, 0), (2, 1))
PARTNER = ((0, 0), (0, 1), (3, 0), (3, 1), (2, 0), (2, 1), (1, 0), (1, 1))
F, R, W = 64, 16, 512
DEPTH = F + 16
ROWS = DEPTH + R
GROUPS = 16
MESH = pl.DeviceIdType.MESH
bf16, f32 = jnp.bfloat16, jnp.float32


def place(group, x, core):
    y, z = lax.div(group, 4), lax.rem(group, 4)
    return (lax.rem(y, 2) * 4 + x, z * 4 + lax.div(y, 2) * 2 + core)


def step_kernel(points, residual, direction, image, coefs, blk, lhs, acc, kbuf, rs, stat, st1, st2,
                g_send, g_recv, r_send, r_recv, a_send, a_recv, b_send, b_recv):
    row, col = lax.axis_index("row"), lax.axis_index("col")
    x, core = lax.rem(row, 4), lax.rem(col, 2)
    group = (lax.rem(lax.div(col, 2), 2) * 2 + lax.div(row, 4)) * 4 + lax.div(col, 4)
    pos = x * 2 + core

    def own_dev(k, sign):
        dx, dc = OWN[k]
        return place(group, lax.rem(x + (dx if sign > 0 else 4 - dx), 4), lax.rem(core + dc, 2))

    def partner_dev(j):
        dx, dc = PARTNER[j]
        return place(lax.rem(group + 8 - pos, GROUPS), lax.rem(x + dx, 4), lax.rem(core + dc, 2))

    def consumer_dev(j):
        dx, dc = PARTNER[j]
        cx, cc = lax.rem(x + 4 - dx, 4), lax.rem(core + dc, 2)
        return place(lax.rem(group + GROUPS - 8 + cx * 2 + cc, GROUPS), cx, cc)

    def label_dev(m, sign):
        return place(lax.rem(group + (m if sign > 0 else GROUPS - m), GROUPS), x, core)

    barrier = pltpu.get_barrier_semaphore()
    greeted = [own_dev(k, 1) for k in range(1, 8)]
    greeted += [partner_dev(j) for j in range(8)] + [consumer_dev(j) for j in range(8)]
    greeted += [label_dev(m, 1) for m in range(1, GROUPS)]
    for dev in greeted:
        pl.semaphore_signal(barrier, inc=1, device_id=dev, device_id_type=MESH)

    special = 1 - lax.div(pos + 7, 8)
    low = special * (1 - lax.div(group, 8))
    row_id = lax.broadcasted_iota(jnp.int32, (16, W), 0)

    p = points[...].astype(f32)
    half = -0.5 * jnp.sum(p * p, axis=0, keepdims=True)
    hi = half.astype(bf16).astype(f32)
    mid = (half - hi).astype(bf16).astype(f32)
    lo = half - hi - mid
    extra = jnp.where(row_id == 0, hi, jnp.where(row_id == 1, mid, jnp.where(row_id == 2, lo, 1.0)))
    blk[0, 0:F, :] = points[...]
    blk[0, F:DEPTH, :] = jnp.where(row_id < 6, extra, 0.0).astype(bf16)
    blk[0, DEPTH:ROWS, :] = direction[...].astype(bf16)
    acc[...] = jnp.zeros_like(acc)

    pl.semaphore_wait(barrier, len(greeted))

    def gather(slot, dev):
        return pltpu.make_async_remote_copy(
            src_ref=blk.at[0], dst_ref=blk.at[slot], send_sem=g_send.at[slot], recv_sem=g_recv.at[slot],
            device_id=dev, device_id_type=MESH)

    for slot in (8, 1, 2, 3, 9, 10, 11, 12, 13, 14, 15, 4, 5, 6, 7):
        gather(slot, own_dev(slot, -1) if slot < 8 else consumer_dev(slot - 8)).start()

    def arrive(slot):
        gather(slot, own_dev(1, 1)).wait_recv()

    def prepare(k):
        tail = pltpu.roll(blk[k, F:DEPTH, :].astype(f32), 3, 0)
        tail = jnp.where(row_id < 3, 1.0, jnp.where(row_id < 6, tail, 0.0)).astype(bf16)
        lhs[k] = jnp.concatenate([blk[k, 0:F, :], tail], axis=0).T

    def make(i, r, half_at):
        s = jnp.dot(lhs[i], blk[r, 0:DEPTH, :], preferred_element_type=f32)
        kbuf[half_at] = jnp.exp2(s * (math.log2(math.e) / 16.0)).astype(bf16)

    def use_rows(i, r, half_at):
        acc[i] += lax.dot_general(blk[r, DEPTH:ROWS, :], kbuf[half_at], (((1,), (1,)), ((), ())),
                                  preferred_element_type=f32)

    def use_columns(i, r, half_at):
        acc[r] += jnp.dot(blk[i, DEPTH:ROWS, :], kbuf[half_at], preferred_element_type=f32)

    prepare(0)
    make(0, 0, 0)
    use_columns(0, 0, 0)

    def tile(b, u):
        second, bb = lax.div(b, 8), lax.rem(b, 8)
        i_a = low * 4 * lax.div(bb, 4) + u
        r_a = 8 + (1 - low) * bb + low * (2 + lax.rem(bb, 4))
        i_s = 4 * lax.rem(bb, 2) + u
        r_s = lax.rem(i_s + 1 + lax.div(bb, 2), 8)
        i = (1 - second) * i_a + second * ((1 - special) * (4 + u) + special * i_s)
        r = (1 - second) * r_a + second * ((1 - special) * (8 + bb) + special * r_s)
        return i, r

    def give(slot, dev):
        return pltpu.make_async_remote_copy(
            src_ref=acc.at[slot], dst_ref=rs.at[slot], send_sem=r_send.at[slot], recv_sem=r_recv.at[slot],
            device_id=dev, device_id_type=MESH)

    for k in range(1, 4):
        arrive(k)
        prepare(k)
    arrive(8)

    @pl.when(low == 1)
    def _():
        arrive(9)
        arrive(10)

    make(*tile(0, 0), 0)

    def body(b, carry):
        ahead = b + 1 + 2 * low

        @pl.when(ahead < 8)
        def _():
            arrive(8 + ahead)

        @pl.when(b == 7 - 4 * low)
        def _():
            for k in range(4, 8):
                arrive(k)
                prepare(k)

        for j in range(6):
            @pl.when(b == 9 + j)
            def _():
                give(8 + j, partner_dev(j)).start()

        @pl.when(b == 15)
        def _():
            give(14, partner_dev(6)).start()

        @pl.when(b + 100 * special == 8)
        def _():
            for k in range(1, 4):
                give(k, own_dev(k, 1)).start()

        after = b + 1 - lax.div(b + 1, 16)
        for u in range(4):
            make(*(tile(b, u + 1) if u < 3 else tile(after, 0)), (u + 1) % 2)
            i, r = tile(b, u)
            use_rows(i, r, u % 2)
            use_columns(i, r, u % 2)
        return carry

    lax.fori_loop(0, 16 - special, body, 0)

    give(15, partner_dev(7)).start()

    @pl.when(special == 1)
    def _():
        give(14, partner_dev(6)).start()
        for k in range(1, 4):
            give(k, own_dev(k, 1)).start()

    for k in (6, 7, 4, 5):
        give(k, own_dev(k, 1)).start()

    total = direction[...] + acc[0]
    for slot in (8, 9, 10, 11, 12, 13, 14, 1, 2, 3, 15, 4, 5, 6, 7):
        give(slot, own_dev(1, 1)).wait_recv()
        total += rs[slot]
    image[...] = total

    res, dirn = residual[...], direction[...]
    sums = [jnp.sum(v, axis=1, keepdims=True) for v in (res * res, dirn * total, res * total, total * total)]
    lane = lax.broadcasted_iota(jnp.int32, (8, 128), 1)
    packed = jnp.zeros((8, 128), f32)
    for n, v in enumerate(sums):
        packed = jnp.where(lane == n, v[0:8], jnp.where(lane == n + 4, v[8:16], packed))
    stat[0] = packed

    def share(src, dst, send, recv, m, dev):
        return pltpu.make_async_remote_copy(
            src_ref=stat.at[src], dst_ref=dst.at[m], send_sem=send.at[m], recv_sem=recv.at[m],
            device_id=dev, device_id_type=MESH)

    for k in range(1, 8):
        share(0, st1, a_send, a_recv, k, own_dev(k, -1)).start()
    for k in range(1, 8):
        share(0, st1, a_send, a_recv, k, own_dev(1, 1)).wait_recv()
        packed += st1[k]
    stat[1] = packed
    for m in range(1, GROUPS):
        share(1, st2, b_send, b_recv, m, label_dev(m, 1)).start()
    for m in range(1, GROUPS):
        share(1, st2, b_send, b_recv, m, own_dev(1, 1)).wait_recv()
        packed += st2[m]

    def pick(n):
        top = jnp.sum(jnp.where(lane == n, packed, 0.0), axis=1, keepdims=True)
        bottom = jnp.sum(jnp.where(lane == n + 4, packed, 0.0), axis=1, keepdims=True)
        return jnp.broadcast_to(jnp.concatenate([top, bottom], axis=0), (R, W))

    old, curvature, cross, square = (pick(n) for n in range(4))
    step = old / curvature
    new = old + step * (step * square - 2.0 * cross)
    coefs[0] = step
    coefs[1] = new / old

    for slot in range(1, 16):
        gather(slot, own_dev(1, 1)).wait_send()
        give(slot, own_dev(1, 1)).wait_send()
    for k in range(1, 8):
        share(0, st1, a_send, a_recv, k, own_dev(1, 1)).wait_send()
    for m in range(1, GROUPS):
        share(1, st2, b_send, b_recv, m, own_dev(1, 1)).wait_send()


def on_device(points, solution, residual, direction):
    vmem = pl.BlockSpec(memory_space=pltpu.VMEM)
    dma = pltpu.SemaphoreType.DMA
    image, coefs = pl.pallas_call(
        step_kernel,
        out_shape=(jax.ShapeDtypeStruct((R, W), f32), jax.ShapeDtypeStruct((2, R, W), f32)),
        in_specs=[vmem] * 3,
        out_specs=(vmem, vmem),
        scratch_shapes=[
            pltpu.VMEM((16, ROWS, W), bf16),
            pltpu.VMEM((8, W, DEPTH), bf16),
            pltpu.VMEM((16, R, W), f32),
            pltpu.VMEM((2, W, W), bf16),
            pltpu.VMEM((16, R, W), f32),
            pltpu.VMEM((2, 8, 128), f32),
            pltpu.VMEM((8, 8, 128), f32),
            pltpu.VMEM((GROUPS, 8, 128), f32),
            dma((16,)), dma((16,)), dma((16,)), dma((16,)),
            dma((8,)), dma((8,)), dma((GROUPS,)), dma((GROUPS,)),
        ],
        compiler_params=pltpu.CompilerParams(
            collective_id=0, has_side_effects=True, vmem_limit_bytes=48 << 20),
        name="cg_step",
    )(points, residual, direction)
    step, beta = coefs[0], coefs[1]
    residual_next = residual - step * image
    return (solution + step * direction, residual_next, residual_next + beta * direction)


def solution(mesh):
    placed = (P(None, ("row", "col")),) * 4
    return jax.shard_map(on_device, mesh=mesh, in_specs=placed, out_specs=placed[:3], check_vma=False)
```

time: 838 us -> 69.5 us (0.08)
  waiting for transfers between devices: 549 us -> 0 us
  blocking collectives: 128 us -> 0 us
  matrix products: 112 us -> 0 us
  Pallas kernels: 0 us -> 65.5 us
  loops' own time: 16.6 us -> 0 us
  between operations: 13.8 us -> 0.66 us
  other arithmetic: 10.1 us -> 0.65 us
    all_gather x2 -> x0, waiting for transfers between devices: 395 us -> none  [the longest x1 204 us: on_device(): everyone = lax.all_gather(points, ('row', 'col'), axis=1, tiled=True)]
    psum x1 -> x0, waiting for transfers between devices: 152 us -> none  [on_device(): summed = lax.psum(accumulated, ('row', 'col'))]
    psum x2 -> x0, blocking collectives: 128 us -> none  [the longest x1 64 us: on_device(): old_norm = lax.psum(jnp.sum(residual * residual, axis=1), ('row', 'col'))]
    dot_general x60 -> x0, matrix products: 112 us -> none  [the longest x20 42.8 us: one_pair(): lax.dot_general(row_points, col_points, (((0,), (0,)), ((), ())), preferr...]
    pallas_call x0 -> x1, Pallas kernels: none -> 65.5 us  [on_device(): pl.pallas_call(step_kernel, out_shape=(jax.ShapeDtypeStruct((R, W), f32),...]
    another operation x1 -> x0, loops' own time: 16.6 us -> none  [triangle_terms(): lax.fori_loop(0, my_pairs.shape[0], one_pair, jnp.zeros((all_directions.s...]
  transfers between devices with their start and end apart: 3 -> 0, of which waited for: 3 -> 0; matrix products, arithmetic and copies ran while one was open for 1% -> 0% of each run, Pallas kernels for 0% -> 0%
where the time goes in v1:
time: 69.5 us; the launch traced here: 69.2 us
  Pallas kernels  65.5 us (94%)
  local copies, waits for them, and re-layouts  2.35 us (3%)
    pallas_call x1, Pallas kernels, on_device(): pl.pallas_call(step_kernel, out_shape=(jax.ShapeDtypeStruct((R, W), f32),...  65.5 us
    unnamed x8, local copies, waits for them, and re-layouts  2.35 us

profile of v1, /device:TPU:1, one launch (start us, length us, event | category | flops | bytes accessed | tf_op | source)
XLA Modules:
  0.0 69.2 jit_solution(11983065753026691878)
XLA Ops:
  0.6 0.0 copy-start
  0.6 0.7 %copy-done = f32[16,512]{1,0:T(8,128)S(1)} copy-done((f32[16,512]{1,0:T(8,128)S(1)}, f32[16,512]{1,0:T(8,128)}, u32[]{:S(2)}) %copy-start) | copy-done | bytes 32792
  1.4 0.0 copy-start.1
  1.4 0.8 %copy-done.1 = f32[16,512]{1,0:T(8,128)S(1)} copy-done((f32[16,512]{1,0:T(8,128)S(1)}, f32[16,512]{1,0:T(8,128)}, u32[]{:S(2)}) %copy-start.1) | copy-done | bytes 32792
  2.1 0.0 copy-start.2
  2.2 0.8 %copy-done.2 = bf16[64,512]{1,0:T(8,128)(2,1)S(1)} copy-done((bf16[64,512]{1,0:T(8,128)(2,1)S(1)}, bf16[64,512]{1,0:T(8,128)(2,1)}, u32[]{:S(2)}) %copy-start.2) | copy-done | bytes 65560
  3.0 0.0 copy-start.3
  3.0 65.5 %cg_step.1 = (f32[16,512]{1,0:T(8,128)S(1)}, f32[2,16,512]{2,1,0:T(8,128)S(1)}) custom-call(bf16[64,512]{1,0:T(8,128)(2,1)S(1)} %copy-done.2, f32[16,512]{1,0:T(8,128)S(1)} %copy-done.1, f32[16,512]{1,0:T(8,128)S(1)} %copy-done), custom_call_target="tpu_custom_call" | custom-call | tf_op jit(solution)/shard_map/cg_step/pallas_call | solution.py:232
  68.5 0.0 copy-done.3
  68.5 0.7 fusion
Async XLA Ops:
  0.6 0.8 %copy-start = (f32[16,512]{1,0:T(8,128)S(1)}, f32[16,512]{1,0:T(8,128)}, u32[]{:S(2)}) copy-start(f32[16,512]{1,0:T(8,128)} %direction.1) | copy-start | bytes 98308
  1.4 0.8 %copy-start.1 = (f32[16,512]{1,0:T(8,128)S(1)}, f32[16,512]{1,0:T(8,128)}, u32[]{:S(2)}) copy-start(f32[16,512]{1,0:T(8,128)} %residual.1) | copy-start | bytes 98308
  2.1 0.8 %copy-start.2 = (bf16[64,512]{1,0:T(8,128)(2,1)S(1)}, bf16[64,512]{1,0:T(8,128)(2,1)}, u32[]{:S(2)}) copy-start(bf16[64,512]{1,0:T(8,128)(2,1)} %points.1) | copy-start | bytes 196612
  3.0 65.5 %copy-start.3 = (f32[16,512]{1,0:T(8,128)S(1)}, f32[16,512]{1,0:T(8,128)}, u32[]{:S(2)}) copy-start(f32[16,512]{1,0:T(8,128)} %param.5) | copy-start | bytes 98308

commit v2 on v1

v2 whole, which is shorter than its diff:
```python
import math

import jax
import jax.numpy as jnp
from jax import lax
from jax.experimental import pallas as pl
from jax.experimental.pallas import tpu as pltpu
from jax.sharding import PartitionSpec as P

OFFSETS = ((0, 0), (0, 1), (1, 0), (1, 1), (3, 0), (3, 1), (2, 0), (2, 1))
F, R, W = 64, 16, 512
DEPTH = F + 16
ROWS = DEPTH + R
GROUPS = 16
MESH = pl.DeviceIdType.MESH
bf16, f32 = jnp.bfloat16, jnp.float32


def step_kernel(points_hbm, residual_hbm, direction_hbm, image, coefs, points, residual, direction,
                blk, lhs, acc, kbuf, rs, stat, st1, st2,
                in_sem, g_send, g_recv, r_send, r_recv, a_send, a_recv, b_send, b_recv):
    loads = [pltpu.make_async_copy(src, dst, in_sem.at[n]) for n, (src, dst) in enumerate(
        ((points_hbm, points), (direction_hbm, direction), (residual_hbm, residual)))]
    for load in loads:
        load.start()

    row, col = lax.axis_index("row"), lax.axis_index("col")
    x, core = lax.rem(row, 4), lax.rem(col, 2)
    y, z = lax.rem(lax.div(col, 2), 2) * 2 + lax.div(row, 4), lax.div(col, 4)
    group, pos = y * 4 + z, x * 2 + core

    def beside(dev, k, sign=1):
        dx, dc = OFFSETS[k]
        there = lax.rem(x + (dx if sign > 0 else 4 - dx), 4) - x if dx else 0
        return (dev[0] + there, dev[1] + (dc * (1 - 2 * core) if dc else 0))

    def of_group(label):
        gy, gz = lax.div(label, 4), lax.rem(label, 4)
        return (lax.rem(gy, 2) * 4 + x, gz * 4 + lax.div(gy, 2) * 2 + core)

    me = (row, col)
    partner = of_group(lax.rem(group + 8 - pos, GROUPS))
    consumer = of_group(lax.rem(group + 8 + pos, GROUPS))

    barrier = pltpu.get_barrier_semaphore()
    greeted = [beside(me, k) for k in (1, 2, 4, 6)] + [partner, consumer]
    for dev in greeted:
        pl.semaphore_signal(barrier, inc=1, device_id=dev, device_id_type=MESH)

    special = 1 - lax.div(pos + 7, 8)
    upper = special * lax.div(group, 8)
    row_id = lax.broadcasted_iota(jnp.int32, (16, W), 0)

    loads[0].wait()
    p = points[...].astype(f32)
    half = -0.5 * jnp.sum(p * p, axis=0, keepdims=True)
    hi = half.astype(bf16).astype(f32)
    mid = (half - hi).astype(bf16).astype(f32)
    lo = half - hi - mid
    extra = jnp.where(row_id == 0, hi, jnp.where(row_id == 1, mid, jnp.where(row_id == 2, lo, 1.0)))
    blk[0, 0:F, :] = points[...]
    blk[0, F:DEPTH, :] = jnp.where(row_id < 6, extra, 0.0).astype(bf16)
    loads[1].wait()
    blk[0, DEPTH:ROWS, :] = direction[...].astype(bf16)
    loads[2].wait()
    acc[...] = jnp.zeros_like(acc)

    pl.semaphore_wait(barrier, len(greeted))

    def pass_on(src, dst, dev):
        return pltpu.make_async_remote_copy(
            src_ref=blk.at[src], dst_ref=blk.at[dst], send_sem=g_send.at[dst], recv_sem=g_recv.at[dst],
            device_id=dev, device_id_type=MESH)

    pass_on(0, 1, beside(me, 1)).start()
    for k in (2, 4):
        pass_on(0, k, beside(me, k, -1)).start()
    pass_on(0, 8, consumer).start()
    pass_on(0, 6, beside(me, 6)).start()

    def arrive(slot):
        pass_on(0, slot, consumer).wait_recv()

    def prepare(k):
        tail = pltpu.roll(blk[k, F:DEPTH, :].astype(f32), 3, 0)
        tail = jnp.where(row_id < 3, 1.0, jnp.where(row_id < 6, tail, 0.0)).astype(bf16)
        lhs[k] = jnp.concatenate([blk[k, 0:F, :], tail], axis=0).T

    def make(i, r, half_at):
        s = jnp.dot(lhs[i], blk[r, 0:DEPTH, :], preferred_element_type=f32)
        kbuf[half_at] = jnp.exp2(s * (math.log2(math.e) / 16.0)).astype(bf16)

    def use_rows(i, r, half_at):
        acc[i] += lax.dot_general(blk[r, DEPTH:ROWS, :], kbuf[half_at], (((1,), (1,)), ((), ())),
                                  preferred_element_type=f32)

    def use_columns(i, r, half_at):
        acc[r] += jnp.dot(blk[i, DEPTH:ROWS, :], kbuf[half_at], preferred_element_type=f32)

    def own_block(k):
        arrive(k)
        if k in (2, 4, 6):
            pass_on(k, k + 1, beside(me, 1)).start()
        pass_on(k, 8 + k, consumer).start()
        prepare(k)

    prepare(0)
    make(0, 0, 0)
    use_columns(0, 0, 0)

    def tile(b, u):
        second, bb = lax.div(b, 8), lax.rem(b, 8)
        quarter, j4 = lax.div(bb, 4), lax.rem(bb, 4)
        i_a = 4 * (upper + (1 - upper) * quarter) + u
        r_a = 8 + j4 + 4 * upper * quarter
        i_n = 4 * (1 - quarter) + u
        r_n = 12 + j4
        i_s = 4 * lax.rem(bb, 2) + u
        r_s = lax.rem(i_s + 1 + lax.div(bb, 2), 8)
        i = (1 - second) * i_a + second * ((1 - special) * i_n + special * i_s)
        r = (1 - second) * r_a + second * ((1 - special) * r_n + special * r_s)
        return i, r

    def give(slot, dev):
        return pltpu.make_async_remote_copy(
            src_ref=acc.at[slot], dst_ref=rs.at[slot], send_sem=r_send.at[slot], recv_sem=r_recv.at[slot],
            device_id=dev, device_id_type=MESH)

    def give_partner(j):
        give(8 + j, beside(partner, j)).start()

    def give_own(k):
        give(k, beside(me, k)).start()

    for k in (1, 2, 4, 3):
        own_block(k)

    @pl.when(upper == 1)
    def _():
        for k in (5, 6, 7):
            own_block(k)

    arrive(8)
    make(*tile(0, 0), 0)

    def body(b, carry):
        for k in (5, 6, 7):
            @pl.when(b + 100 * upper == k - 5)
            def _():
                own_block(k)

        early = jnp.logical_and(b < 7, jnp.logical_or(b < 3, upper == 1))
        late = jnp.logical_and(jnp.logical_and(b >= 7, b < 11), upper == 0)

        @pl.when(early)
        def _():
            arrive(9 + b)

        @pl.when(late)
        def _():
            arrive(5 + b)

        for j in range(7):
            @pl.when(b == (6 + j if j < 4 else 9 + j))
            def _():
                give_partner(j)

        @pl.when(b + 100 * special == 12)
        def _():
            for k in (6, 7, 4, 5):
                give_own(k)

        after = b + 1 - lax.div(b + 1, 16)
        for u in range(4):
            make(*(tile(b, u + 1) if u < 3 else tile(after, 0)), (u + 1) % 2)
            i, r = tile(b, u)
            use_rows(i, r, u % 2)
            use_columns(i, r, u % 2)
        return carry

    lax.fori_loop(0, 16 - special, body, 0)

    @pl.when(special == 1)
    def _():
        for k in (6, 7, 4, 5):
            give_own(k)
        give_partner(6)

    give_partner(7)
    for k in (2, 3, 1):
        give_own(k)

    total = direction[...] + acc[0]
    for slot in (8, 9, 10, 11, 12, 13, 6, 7, 4, 5, 14, 15, 1, 2, 3):
        give(slot, me).wait_recv()
        total += rs[slot]
    image[...] = total

    res, dirn = residual[...], direction[...]
    sums = [jnp.sum(v, axis=1, keepdims=True) for v in (res * res, dirn * total, res * total, total * total)]
    lane = lax.broadcasted_iota(jnp.int32, (8, 128), 1)
    packed = jnp.zeros((8, 128), f32)
    for n, v in enumerate(sums):
        packed = jnp.where(lane == n, v[0:8], jnp.where(lane == n + 4, v[8:16], packed))
    stat[0] = packed

    def share(src, dst, send, recv, m, dev):
        return pltpu.make_async_remote_copy(
            src_ref=stat.at[src], dst_ref=dst.at[m], send_sem=send.at[m], recv_sem=recv.at[m],
            device_id=dev, device_id_type=MESH)

    for k in (6, 7, 2, 3, 4, 5, 1):
        share(0, st1, a_send, a_recv, k, beside(me, k, -1)).start()
    ys = [lax.rem(y + d, 4) for d in range(4)]
    zs = [lax.rem(z + d, 4) * 4 for d in range(4)]
    rows = [lax.rem(v, 2) * 4 + x for v in ys]
    cols = [lax.div(v, 2) * 2 + core for v in ys]
    for k in (1, 2, 3, 4, 5, 6, 7):
        share(0, st1, a_send, a_recv, k, me).wait_recv()
        packed += st1[k]
    stat[1] = packed
    order = (10, 6, 14, 9, 11, 2, 8, 5, 7, 13, 15, 1, 3, 4, 12)
    for m in order:
        share(1, st2, b_send, b_recv, m, (rows[m // 4], cols[m // 4] + zs[m % 4])).start()
    for m in reversed(order):
        share(1, st2, b_send, b_recv, m, me).wait_recv()
        packed += st2[m]

    def pick(n):
        top = jnp.sum(jnp.where(lane == n, packed, 0.0), axis=1, keepdims=True)
        bottom = jnp.sum(jnp.where(lane == n + 4, packed, 0.0), axis=1, keepdims=True)
        return jnp.broadcast_to(jnp.concatenate([top, bottom], axis=0), (R, W))

    old, curvature, cross, square = (pick(n) for n in range(4))
    step = old / curvature
    new = old + step * (step * square - 2.0 * cross)
    coefs[0] = step
    coefs[1] = new / old

    for slot in range(1, 16):
        pass_on(0, slot, consumer).wait_send()
        give(slot, me).wait_send()
    for k in range(1, 8):
        share(0, st1, a_send, a_recv, k, me).wait_send()
    for m in range(1, GROUPS):
        share(1, st2, b_send, b_recv, m, me).wait_send()


def on_device(points, solution, residual, direction):
    vmem = pl.BlockSpec(memory_space=pltpu.VMEM)
    dma = pltpu.SemaphoreType.DMA
    image, coefs = pl.pallas_call(
        step_kernel,
        out_shape=(jax.ShapeDtypeStruct((R, W), f32), jax.ShapeDtypeStruct((2, R, W), f32)),
        in_specs=[pl.BlockSpec(memory_space=pltpu.HBM)] * 3,
        out_specs=(vmem, vmem),
        scratch_shapes=[
            pltpu.VMEM((F, W), bf16),
            pltpu.VMEM((R, W), f32),
            pltpu.VMEM((R, W), f32),
            pltpu.VMEM((16, ROWS, W), bf16),
            pltpu.VMEM((8, W, DEPTH), bf16),
            pltpu.VMEM((16, R, W), f32),
            pltpu.VMEM((2, W, W), bf16),
            pltpu.VMEM((16, R, W), f32),
            pltpu.VMEM((2, 8, 128), f32),
            pltpu.VMEM((8, 8, 128), f32),
            pltpu.VMEM((GROUPS, 8, 128), f32),
            dma((3,)), dma((16,)), dma((16,)), dma((16,)), dma((16,)),
            dma((8,)), dma((8,)), dma((GROUPS,)), dma((GROUPS,)),
        ],
        compiler_params=pltpu.CompilerParams(
            collective_id=0, has_side_effects=True, vmem_limit_bytes=48 << 20),
        name="cg_step",
    )(points, residual, direction)
    step, beta = coefs[0], coefs[1]
    residual_next = residual - step * image
    return (solution + step * direction, residual_next, residual_next + beta * direction)


def solution(mesh):
    placed = (P(None, ("row", "col")),) * 4
    return jax.shard_map(on_device, mesh=mesh, in_specs=placed, out_specs=placed[:3], check_vma=False)
```

time: 69.5 us -> 59.2 us (0.85)
  Pallas kernels: 65.5 us -> 55.3 us
    pallas_call x1, Pallas kernels: 65.5 us -> 55.3 us  [on_device(): pl.pallas_call(step_kernel, out_shape=(jax.ShapeDtypeStruct((R, W), f32),...]
where the time goes in v2:
time: 59.2 us; the launch traced here: 58.9 us
  Pallas kernels  55.3 us (93%)
  local copies, waits for them, and re-layouts  2.35 us (4%)
  between operations  0.66 us (1%)
  other arithmetic  0.65 us (1%)
    pallas_call x1, Pallas kernels, on_device(): pl.pallas_call(step_kernel, out_shape=(jax.ShapeDtypeStruct((R, W), f32),...  55.3 us
    unnamed x8, local copies, waits for them, and re-layouts  2.35 us

profile of v2, /device:TPU:1, one launch (start us, length us, event | category | flops | bytes accessed | tf_op | source)
XLA Modules:
  0.0 58.9 jit_solution(15990172648384346522)
XLA Ops:
  0.6 0.0 copy-start
  0.6 0.7 %copy-done = f32[16,512]{1,0:T(8,128)S(1)} copy-done((f32[16,512]{1,0:T(8,128)S(1)}, f32[16,512]{1,0:T(8,128)}, u32[]{:S(2)}) %copy-start) | copy-done | bytes 32792
  1.4 0.0 copy-start.1
  1.4 0.8 %copy-done.1 = f32[16,512]{1,0:T(8,128)S(1)} copy-done((f32[16,512]{1,0:T(8,128)S(1)}, f32[16,512]{1,0:T(8,128)}, u32[]{:S(2)}) %copy-start.1) | copy-done | bytes 32792
  2.1 0.0 copy-start.2
  2.2 0.8 %copy-done.2 = bf16[64,512]{1,0:T(8,128)(2,1)S(1)} copy-done((bf16[64,512]{1,0:T(8,128)(2,1)S(1)}, bf16[64,512]{1,0:T(8,128)(2,1)}, u32[]{:S(2)}) %copy-start.2) | copy-done | bytes 65560
  3.0 0.0 copy-start.3
  3.0 55.3 %cg_step.1 = (f32[16,512]{1,0:T(8,128)S(1)}, f32[2,16,512]{2,1,0:T(8,128)S(1)}) custom-call(bf16[64,512]{1,0:T(8,128)(2,1)S(1)} %copy-done.2, f32[16,512]{1,0:T(8,128)S(1)} %copy-done.1, f32[16,512]{1,0:T(8,128)S(1)} %copy-done), custom_call_target="tpu_custom_call" | custom-call | tf_op jit(solution)/shard_map/cg_step/pallas_call | solution.py:252
  58.3 0.0 copy-done.3
  58.3 0.7 %fusion = (f32[16,512]{1,0:T(8,128)}, f32[16,512]{1,0:T(8,128)}, f32[16,512]{1,0:T(8,128)}) fusion(f32[16,512]{1,0:T(8,128)S(1)} %copy-done, f32[2,16,512]{2,1,0:T(8,128)S(1)} %get-tuple-element.5, f32[16,512]{1,0:T(8,128)S(1)} %copy-done.1, f32[16,512]{1,0:T(8,128)S(1)} %get-tuple-element.6, f32[16,512]{1,0:T(8,128)S(1)} %copy-done.3), kind=kLoop, calls=%fused_computation.1 | loop fusion | flops 49152 | bytes 294912 | tf_op jit(solution)/shard_map/add | solution.py:278
Async XLA Ops:
  0.6 0.8 %copy-start = (f32[16,512]{1,0:T(8,128)S(1)}, f32[16,512]{1,0:T(8,128)}, u32[]{:S(2)}) copy-start(f32[16,512]{1,0:T(8,128)} %direction_hbm.1) | copy-start | bytes 98308
  1.4 0.8 %copy-start.1 = (f32[16,512]{1,0:T(8,128)S(1)}, f32[16,512]{1,0:T(8,128)}, u32[]{:S(2)}) copy-start(f32[16,512]{1,0:T(8,128)} %residual_hbm.1) | copy-start | bytes 98308
  2.1 0.8 %copy-start.2 = (bf16[64,512]{1,0:T(8,128)(2,1)S(1)}, bf16[64,512]{1,0:T(8,128)(2,1)}, u32[]{:S(2)}) copy-start(bf16[64,512]{1,0:T(8,128)(2,1)} %points_hbm.1) | copy-start | bytes 196612
  3.0 55.3 %copy-start.3 = (f32[16,512]{1,0:T(8,128)S(1)}, f32[16,512]{1,0:T(8,128)}, u32[]{:S(2)}) copy-start(f32[16,512]{1,0:T(8,128)} %param.5) | copy-start | bytes 98308

commit v3 on v2

--- a/solution.py
+++ b/solution.py
@@ -7,7 +7,10 @@
 from jax.experimental.pallas import tpu as pltpu
 from jax.sharding import PartitionSpec as P
 
-OFFSETS = ((0, 0), (0, 1), (1, 0), (1, 1), (3, 0), (3, 1), (2, 0), (2, 1))
+OFFSETS = ((0, 0), (0, 1), (1, 0), (3, 0), (2, 0), (2, 1), (1, 1), (3, 1))
+SIBLING = 1
+RELAYED = {2: 6, 3: 7, 4: 5}
+SHIFT = ((2, 2), (1, 1), (1, 2), (3, 0), (2, 1), (0, 3), (0, 0), (1, 3))
 F, R, W = 64, 16, 512
 DEPTH = F + 16
 ROWS = DEPTH + R
@@ -27,28 +30,35 @@
     row, col = lax.axis_index("row"), lax.axis_index("col")
     x, core = lax.rem(row, 4), lax.rem(col, 2)
     y, z = lax.rem(lax.div(col, 2), 2) * 2 + lax.div(row, 4), lax.div(col, 4)
-    group, pos = y * 4 + z, x * 2 + core
+    pos = x * 2 + core
 
     def beside(dev, k, sign=1):
         dx, dc = OFFSETS[k]
         there = lax.rem(x + (dx if sign > 0 else 4 - dx), 4) - x if dx else 0
         return (dev[0] + there, dev[1] + (dc * (1 - 2 * core) if dc else 0))
 
-    def of_group(label):
-        gy, gz = lax.div(label, 4), lax.rem(label, 4)
+    def choose(values):
+        return sum(jnp.where(pos == n, v, 0) for n, v in enumerate(values) if v)
+
+    def moved(dy, dz):
+        gy, gz = lax.rem(y + dy, 4), lax.rem(z + dz, 4)
         return (lax.rem(gy, 2) * 4 + x, gz * 4 + lax.div(gy, 2) * 2 + core)
 
     me = (row, col)
-    partner = of_group(lax.rem(group + 8 - pos, GROUPS))
-    consumer = of_group(lax.rem(group + 8 + pos, GROUPS))
+    turn = lax.rem(lax.div(y, 2) + lax.div(z, 2), 2)
+    square = choose((0,) * 6 + (2, 0))
+    shift_y, shift_z = choose([v[0] for v in SHIFT]), choose([v[1] for v in SHIFT])
+    partner = moved(shift_y + square * (1 - turn), shift_z + square * turn)
+    consumer = moved(4 - shift_y - square * turn, 4 - shift_z - square * (1 - turn))
 
     barrier = pltpu.get_barrier_semaphore()
-    greeted = [beside(me, k) for k in (1, 2, 4, 6)] + [partner, consumer]
+    greeted = [beside(me, k) for k in (SIBLING, 2, 3, 4)] + [partner, consumer]
     for dev in greeted:
         pl.semaphore_signal(barrier, inc=1, device_id=dev, device_id_type=MESH)
 
     special = 1 - lax.div(pos + 7, 8)
-    upper = special * lax.div(group, 8)
+    upper = special * lax.div(y, 2)
+    normal = 1 - special
     row_id = lax.broadcasted_iota(jnp.int32, (16, W), 0)
 
     loads[0].wait()
@@ -72,11 +82,11 @@
             src_ref=blk.at[src], dst_ref=blk.at[dst], send_sem=g_send.at[dst], recv_sem=g_recv.at[dst],
             device_id=dev, device_id_type=MESH)
 
-    pass_on(0, 1, beside(me, 1)).start()
-    for k in (2, 4):
+    for k in (2, 3):
         pass_on(0, k, beside(me, k, -1)).start()
     pass_on(0, 8, consumer).start()
-    pass_on(0, 6, beside(me, 6)).start()
+    pass_on(0, SIBLING, beside(me, SIBLING)).start()
+    pass_on(0, 4, beside(me, 4)).start()
 
     def arrive(slot):
         pass_on(0, slot, consumer).wait_recv()
@@ -99,26 +109,33 @@
 
     def own_block(k):
         arrive(k)
-        if k in (2, 4, 6):
-            pass_on(k, k + 1, beside(me, 1)).start()
+        if k in RELAYED:
+            pass_on(k, RELAYED[k], beside(me, SIBLING)).start()
+
+    def forward(k):
         pass_on(k, 8 + k, consumer).start()
-        prepare(k)
 
     prepare(0)
     make(0, 0, 0)
     use_columns(0, 0, 0)
 
     def tile(b, u):
-        second, bb = lax.div(b, 8), lax.rem(b, 8)
-        quarter, j4 = lax.div(bb, 4), lax.rem(bb, 4)
-        i_a = 4 * (upper + (1 - upper) * quarter) + u
-        r_a = 8 + j4 + 4 * upper * quarter
-        i_n = 4 * (1 - quarter) + u
-        r_n = 12 + j4
-        i_s = 4 * lax.rem(bb, 2) + u
-        r_s = lax.rem(i_s + 1 + lax.div(bb, 2), 8)
-        i = (1 - second) * i_a + second * ((1 - special) * i_n + special * i_s)
-        r = (1 - second) * r_a + second * ((1 - special) * r_n + special * r_s)
+        half, parity = lax.div(b, 2), lax.rem(b, 2)
+        swap = special * (lax.div(b + 3, 16) - lax.div(b + 1, 16))
+        half_s = half + swap * parity
+        parity_s = parity + swap * (1 - 2 * parity)
+        half_s = half_s - swap * (1 - parity)
+        first, start = 1 - lax.div(b + 14, 16), 1 - lax.div(b + 12, 16)
+        cross = start - first
+        i_n = (1 - start) * 4 * (1 - parity) + cross * (6 - 2 * parity) + (1 - cross) * u + cross * (u % 2)
+        j_n = first * parity + cross * (u // 2) + (1 - start) * half
+        hh, pair = lax.rem(half_s, 2), lax.div(half_s, 2)
+        i_p = 4 * hh + upper * 2 * (u % 2) + (1 - upper) * u
+        j_p = 2 * pair + upper * (u // 2) + (1 - upper)
+        i_s = 4 * hh + u
+        r_s = lax.rem(i_s + 1 + pair, 8)
+        i = normal * i_n + special * ((1 - parity_s) * i_p + parity_s * i_s)
+        r = normal * (8 + j_n) + special * ((1 - parity_s) * (8 + j_p) + parity_s * r_s)
         return i, r
 
     def give(slot, dev):
@@ -132,66 +149,95 @@
     def give_own(k):
         give(k, beside(me, k)).start()
 
-    for k in (1, 2, 4, 3):
+    own_block(1)
+    forward(1)
+    prepare(1)
+    for k in (2, 3):
         own_block(k)
-
-    @pl.when(upper == 1)
+    for k in (2, 3):
+        forward(k)
+        prepare(k)
+    arrive(8)
+
+    @pl.when(special == 1)
     def _():
-        for k in (5, 6, 7):
-            own_block(k)
-
-    arrive(8)
-    make(*tile(0, 0), 0)
-
-    def body(b, carry):
-        for k in (5, 6, 7):
-            @pl.when(b + 100 * upper == k - 5)
-            def _():
-                own_block(k)
-
-        early = jnp.logical_and(b < 7, jnp.logical_or(b < 3, upper == 1))
-        late = jnp.logical_and(jnp.logical_and(b >= 7, b < 11), upper == 0)
-
-        @pl.when(early)
-        def _():
-            arrive(9 + b)
-
-        @pl.when(late)
-        def _():
-            arrive(5 + b)
-
-        for j in range(7):
-            @pl.when(b == (6 + j if j < 4 else 9 + j))
-            def _():
-                give_partner(j)
-
-        @pl.when(b + 100 * special == 12)
-        def _():
-            for k in (6, 7, 4, 5):
-                give_own(k)
-
-        after = b + 1 - lax.div(b + 1, 16)
-        for u in range(4):
-            make(*(tile(b, u + 1) if u < 3 else tile(after, 0)), (u + 1) % 2)
+        arrive(9)
+
+    def work(b, b_next, us):
+        for u in us:
+            make(*(tile(b, u + 1) if u < 3 else tile(b_next, 0)), (u + 1) % 2)
             i, r = tile(b, u)
             use_rows(i, r, u % 2)
             use_columns(i, r, u % 2)
+
+    make(*tile(0, 0), 0)
+    work(0, 0, range(3))
+
+    @pl.when(special == 0)
+    def _():
+        arrive(9)
+
+    work(0, 1, (3,))
+
+    def body(b, carry):
+        @pl.when(b == 1)
+        def _():
+            for k in (6, 7):
+                own_block(k)
+                prepare(k)
+
+        @pl.when(b == 2 - special)
+        def _():
+            own_block(4)
+            forward(4)
+            prepare(4)
+
+        @pl.when(b == 3 - special)
+        def _():
+            own_block(5)
+            prepare(5)
+            for k in (5, 6, 7):
+                forward(k)
+
+        for j in range(2, 8):
+            @pl.when(b == normal * (2 * j - 1) + special * (4 * (j // 2) - 1))
+            def _():
+                arrive(8 + j)
+
+        for j in range(7):
+            @pl.when(b == (2 * j + 3 if j else 4))
+            def _():
+                give_partner(j)
+
+        @pl.when(b == 14 + 100 * (1 - special))
+        def _():
+            give_partner(6)
+            give_partner(7)
+
+        @pl.when(b + 100 * special == 15)
+        def _():
+            for k in (4, 5, 6, 7):
+                give_own(k)
+
+        work(b, b + 1 - lax.div(b + 1, 16), range(4))
         return carry
 
-    lax.fori_loop(0, 16 - special, body, 0)
+    lax.fori_loop(1, 16 - special, body, 0)
 
     @pl.when(special == 1)
     def _():
-        for k in (6, 7, 4, 5):
+        for k in (4, 5, 6, 7):
             give_own(k)
-        give_partner(6)
-
-    give_partner(7)
+
+    @pl.when(special == 0)
+    def _():
+        give_partner(7)
+
     for k in (2, 3, 1):
         give_own(k)
 
     total = direction[...] + acc[0]
-    for slot in (8, 9, 10, 11, 12, 13, 6, 7, 4, 5, 14, 15, 1, 2, 3):
+    for slot in (8, 9, 10, 11, 12, 13, 14, 6, 7, 4, 5, 1, 2, 3, 15):
         give(slot, me).wait_recv()
         total += rs[slot]
     image[...] = total
@@ -209,13 +255,13 @@
             src_ref=stat.at[src], dst_ref=dst.at[m], send_sem=send.at[m], recv_sem=recv.at[m],
             device_id=dev, device_id_type=MESH)
 
-    for k in (6, 7, 2, 3, 4, 5, 1):
+    for k in (4, 5, 2, 3, 6, 7, 1):
         share(0, st1, a_send, a_recv, k, beside(me, k, -1)).start()
     ys = [lax.rem(y + d, 4) for d in range(4)]
     zs = [lax.rem(z + d, 4) * 4 for d in range(4)]
     rows = [lax.rem(v, 2) * 4 + x for v in ys]
     cols = [lax.div(v, 2) * 2 + core for v in ys]
-    for k in (1, 2, 3, 4, 5, 6, 7):
+    for k in (1, 2, 3, 6, 7, 4, 5):
         share(0, st1, a_send, a_recv, k, me).wait_recv()
         packed += st1[k]
     stat[1] = packed
@@ -270,7 +316,7 @@
             dma((8,)), dma((8,)), dma((GROUPS,)), dma((GROUPS,)),
         ],
         compiler_params=pltpu.CompilerParams(
-            collective_id=0, has_side_effects=True, vmem_limit_bytes=48 << 20),
+            collective_id=0, has_side_effects=True, vmem_limit_bytes=67000000),
         name="cg_step",
     )(points, residual, direction)
     step, beta = coefs[0], coefs[1]

time: 59.2 us -> 54.1 us (0.914)
  Pallas kernels: 55.3 us -> 51.5 us
  local copies, waits for them, and re-layouts: 2.35 us -> 0.01 us
  other arithmetic: 0.65 us -> 1.48 us
    pallas_call x1, Pallas kernels: 55.3 us -> 51.5 us  [on_device(): pl.pallas_call(step_kernel, out_shape=(jax.ShapeDtypeStruct((R, W), f32),...]
    unnamed x8 -> x2, local copies, waits for them, and re-layouts: 2.35 us -> 0.01 us
    add x1, other arithmetic: 0.65 us -> 1.48 us  [on_device(): residual_next + beta * direction]
where the time goes in v3:
time: 54.1 us; the launch traced here: 53.6 us
  Pallas kernels  51.5 us (95%)
  other arithmetic  1.48 us (3%)
  between operations  0.65 us (1%)
    pallas_call x1, Pallas kernels, on_device(): pl.pallas_call(step_kernel, out_shape=(jax.ShapeDtypeStruct((R, W), f32),...  51.5 us
    add x1, other arithmetic, on_device(): residual_next + beta * direction  1.48 us

profile of v3, /device:TPU:1, one launch (start us, length us, event | category | flops | bytes accessed | tf_op | source)
XLA Modules:
  0.0 53.6 jit_solution(7791906043597591946)
XLA Ops:
  0.6 0.0 copy-start
  0.6 51.5 %cg_step.1 = (f32[16,512]{1,0:T(8,128)}, f32[2,16,512]{2,1,0:T(8,128)}) custom-call(bf16[64,512]{1,0:T(8,128)(2,1)} %points_hbm.1, f32[16,512]{1,0:T(8,128)} %residual_hbm.1, f32[16,512]{1,0:T(8,128)} %direction_hbm.1), custom_call_target="tpu_custom_call" | custom-call | tf_op jit(solution)/shard_map/cg_step/pallas_call | solution.py:298
  52.1 0.0 copy-done
  52.2 1.5 %fusion = (f32[16,512]{1,0:T(8,128)}, f32[16,512]{1,0:T(8,128)}, f32[16,512]{1,0:T(8,128)}) fusion(f32[16,512]{1,0:T(8,128)S(1)} %copy-done, f32[2,16,512]{2,1,0:T(8,128)} %get-tuple-element.5, f32[16,512]{1,0:T(8,128)} %residual_hbm.1, f32[16,512]{1,0:T(8,128)} %get-tuple-element.6, f32[16,512]{1,0:T(8,128)} %param.5), kind=kLoop, calls=%fused_computation.1 | loop fusion | flops 49152 | bytes 294912 | tf_op jit(solution)/shard_map/add | solution.py:324
Async XLA Ops:
  0.6 51.5 %copy-start = (f32[16,512]{1,0:T(8,128)S(1)}, f32[16,512]{1,0:T(8,128)}, u32[]{:S(2)}) copy-start(f32[16,512]{1,0:T(8,128)} %direction_hbm.1) | copy-start | bytes 98308

commit v4 on v3

--- a/solution.py
+++ b/solution.py
@@ -12,8 +12,9 @@
 RELAYED = {2: 6, 3: 7, 4: 5}
 SHIFT = ((2, 2), (1, 1), (1, 2), (3, 0), (2, 1), (0, 3), (0, 0), (1, 3))
 F, R, W = 64, 16, 512
+SENT = R + F
 DEPTH = F + 16
-ROWS = DEPTH + R
+ROWS = SENT + 16
 GROUPS = 16
 MESH = pl.DeviceIdType.MESH
 bf16, f32 = jnp.bfloat16, jnp.float32
@@ -58,62 +59,71 @@
 
     special = 1 - lax.div(pos + 7, 8)
     upper = special * lax.div(y, 2)
+    lower = special - upper
     normal = 1 - special
     row_id = lax.broadcasted_iota(jnp.int32, (16, W), 0)
 
-    loads[0].wait()
-    p = points[...].astype(f32)
-    half = -0.5 * jnp.sum(p * p, axis=0, keepdims=True)
-    hi = half.astype(bf16).astype(f32)
-    mid = (half - hi).astype(bf16).astype(f32)
-    lo = half - hi - mid
-    extra = jnp.where(row_id == 0, hi, jnp.where(row_id == 1, mid, jnp.where(row_id == 2, lo, 1.0)))
-    blk[0, 0:F, :] = points[...]
-    blk[0, F:DEPTH, :] = jnp.where(row_id < 6, extra, 0.0).astype(bf16)
-    loads[1].wait()
-    blk[0, DEPTH:ROWS, :] = direction[...].astype(bf16)
-    loads[2].wait()
+    def extend(slot):
+        p = blk[slot, R:SENT, :].astype(f32)
+        half = -0.5 * jnp.sum(p * p, axis=0, keepdims=True)
+        hi = half.astype(bf16).astype(f32)
+        mid = (half - hi).astype(bf16).astype(f32)
+        lo = half - hi - mid
+        pieces = jnp.where(row_id == 0, hi, jnp.where(row_id == 1, mid, jnp.where(row_id == 2, lo, 1.0)))
+        blk[slot, SENT:ROWS, :] = jnp.where(row_id < 6, pieces, 0.0).astype(bf16)
+
+    for load in loads:
+        load.wait()
+    blk[0, 0:R, :] = direction[...].astype(bf16)
+    blk[0, R:SENT, :] = points[...]
+    extend(0)
     acc[...] = jnp.zeros_like(acc)
 
     pl.semaphore_wait(barrier, len(greeted))
 
     def pass_on(src, dst, dev):
         return pltpu.make_async_remote_copy(
-            src_ref=blk.at[src], dst_ref=blk.at[dst], send_sem=g_send.at[dst], recv_sem=g_recv.at[dst],
+            src_ref=blk.at[src, pl.ds(0, SENT)], dst_ref=blk.at[dst, pl.ds(0, SENT)], send_sem=g_send.at[dst], recv_sem=g_recv.at[dst],
             device_id=dev, device_id_type=MESH)
 
+    def forward(k):
+        if k % 2:
+            pass_on(k, 8 + k, consumer).start()
+        else:
+            @pl.when(upper == 0)
+            def _():
+                pass_on(k, 8 + k, consumer).start()
+
+    forward(0)
     for k in (2, 3):
         pass_on(0, k, beside(me, k, -1)).start()
-    pass_on(0, 8, consumer).start()
     pass_on(0, SIBLING, beside(me, SIBLING)).start()
     pass_on(0, 4, beside(me, 4)).start()
 
     def arrive(slot):
         pass_on(0, slot, consumer).wait_recv()
+        extend(slot)
 
     def prepare(k):
-        tail = pltpu.roll(blk[k, F:DEPTH, :].astype(f32), 3, 0)
+        tail = pltpu.roll(blk[k, SENT:ROWS, :].astype(f32), 3, 0)
         tail = jnp.where(row_id < 3, 1.0, jnp.where(row_id < 6, tail, 0.0)).astype(bf16)
-        lhs[k] = jnp.concatenate([blk[k, 0:F, :], tail], axis=0).T
+        lhs[k] = jnp.concatenate([blk[k, R:SENT, :], tail], axis=0).T
 
     def make(i, r, half_at):
-        s = jnp.dot(lhs[i], blk[r, 0:DEPTH, :], preferred_element_type=f32)
+        s = jnp.dot(lhs[i], blk[r, R:ROWS, :], preferred_element_type=f32)
         kbuf[half_at] = jnp.exp2(s * (math.log2(math.e) / 16.0)).astype(bf16)
 
     def use_rows(i, r, half_at):
-        acc[i] += lax.dot_general(blk[r, DEPTH:ROWS, :], kbuf[half_at], (((1,), (1,)), ((), ())),
+        acc[i] += lax.dot_general(blk[r, 0:R, :], kbuf[half_at], (((1,), (1,)), ((), ())),
                                   preferred_element_type=f32)
 
     def use_columns(i, r, half_at):
-        acc[r] += jnp.dot(blk[i, DEPTH:ROWS, :], kbuf[half_at], preferred_element_type=f32)
+        acc[r] += jnp.dot(blk[i, 0:R, :], kbuf[half_at], preferred_element_type=f32)
 
     def own_block(k):
         arrive(k)
         if k in RELAYED:
             pass_on(k, RELAYED[k], beside(me, SIBLING)).start()
-
-    def forward(k):
-        pass_on(k, 8 + k, consumer).start()
 
     prepare(0)
     make(0, 0, 0)
@@ -125,10 +135,10 @@
         half_s = half + swap * parity
         parity_s = parity + swap * (1 - 2 * parity)
         half_s = half_s - swap * (1 - parity)
-        first, start = 1 - lax.div(b + 14, 16), 1 - lax.div(b + 12, 16)
-        cross = start - first
-        i_n = (1 - start) * 4 * (1 - parity) + cross * (6 - 2 * parity) + (1 - cross) * u + cross * (u % 2)
-        j_n = first * parity + cross * (u // 2) + (1 - start) * half
+        early, zero, last = 1 - lax.div(b + 13, 16), 1 - lax.div(b + 15, 16), lax.div(b + 1, 16)
+        cross = early - zero
+        i_n = cross * (8 - 2 * b + u % 2) + (1 - cross) * (4 * parity * (1 - last) + u)
+        j_n = cross * (u // 2) + (1 - early) * ((1 - last) * lax.div(b + 1, 2) + last)
         hh, pair = lax.rem(half_s, 2), lax.div(half_s, 2)
         i_p = 4 * hh + upper * 2 * (u % 2) + (1 - upper) * u
         j_p = 2 * pair + upper * (u // 2) + (1 - upper)
@@ -157,7 +167,10 @@
     for k in (2, 3):
         forward(k)
         prepare(k)
-    arrive(8)
+
+    @pl.when(lower == 0)
+    def _():
+        arrive(8)
 
     @pl.when(special == 1)
     def _():
@@ -173,26 +186,24 @@
     make(*tile(0, 0), 0)
     work(0, 0, range(3))
 
-    @pl.when(special == 0)
-    def _():
-        arrive(9)
+    for k in (6, 7):
+        own_block(k)
+        prepare(k)
 
     work(0, 1, (3,))
 
     def body(b, carry):
         @pl.when(b == 1)
-        def _():
-            for k in (6, 7):
-                own_block(k)
-                prepare(k)
-
-        @pl.when(b == 2 - special)
         def _():
             own_block(4)
             forward(4)
             prepare(4)
 
-        @pl.when(b == 3 - special)
+            @pl.when(special == 0)
+            def _():
+                arrive(9)
+
+        @pl.when(b == 2)
         def _():
             own_block(5)
             prepare(5)
@@ -200,21 +211,16 @@
                 forward(k)
 
         for j in range(2, 8):
-            @pl.when(b == normal * (2 * j - 1) + special * (4 * (j // 2) - 1))
+            @pl.when(b == normal * (2 * j - 2) + special * (4 * (j // 2) - 1) + (0 if j % 2 else 100 * lower))
             def _():
                 arrive(8 + j)
 
-        for j in range(7):
-            @pl.when(b == (2 * j + 3 if j else 4))
+        for j, at in ((0, 4), (1, 5 + 100 * normal), (2, 7), (3, 8), (4, 11), (5, 12), (6, 14), (7, 14 + normal)):
+            @pl.when(b == at)
             def _():
                 give_partner(j)
 
-        @pl.when(b == 14 + 100 * (1 - special))
-        def _():
-            give_partner(6)
-            give_partner(7)
-
-        @pl.when(b + 100 * special == 15)
+        @pl.when(b + 100 * special == 14)
         def _():
             for k in (4, 5, 6, 7):
                 give_own(k)
@@ -231,13 +237,13 @@
 
     @pl.when(special == 0)
     def _():
-        give_partner(7)
+        give_partner(1)
 
     for k in (2, 3, 1):
         give_own(k)
 
     total = direction[...] + acc[0]
-    for slot in (8, 9, 10, 11, 12, 13, 14, 6, 7, 4, 5, 1, 2, 3, 15):
+    for slot in (8, 10, 11, 12, 13, 14, 15, 6, 7, 4, 5, 1, 2, 3, 9):
         give(slot, me).wait_recv()
         total += rs[slot]
     image[...] = total
@@ -284,8 +290,15 @@
     coefs[1] = new / old
 
     for slot in range(1, 16):
-        pass_on(0, slot, consumer).wait_send()
+        if slot < 8 or slot % 2:
+            pass_on(0, slot, consumer).wait_send()
         give(slot, me).wait_send()
+
+    @pl.when(upper == 0)
+    def _():
+        for slot in (8, 10, 12, 14):
+            pass_on(0, slot, consumer).wait_send()
+
     for k in range(1, 8):
         share(0, st1, a_send, a_recv, k, me).wait_send()
     for m in range(1, GROUPS):

time: 54.1 us -> 53.4 us (0.987)
  no operation moved by 1% of the time
where the time goes in v4:
time: 53.4 us; the launch traced here: 53.2 us
  Pallas kernels  51 us (96%)
  other arithmetic  1.48 us (3%)
  between operations  0.65 us (1%)
    pallas_call x1, Pallas kernels, on_device(): pl.pallas_call(step_kernel, out_shape=(jax.ShapeDtypeStruct((R, W), f32),...  51 us
    add x1, other arithmetic, on_device(): residual_next + beta * direction  1.48 us

profile of v4, /device:TPU:1, one launch (start us, length us, event | category | flops | bytes accessed | tf_op | source)
XLA Modules:
  0.0 53.2 jit_solution(5019805183588388906)
XLA Ops:
  0.6 0.0 copy-start
  0.6 51.0 %cg_step.1 = (f32[16,512]{1,0:T(8,128)}, f32[2,16,512]{2,1,0:T(8,128)}) custom-call(bf16[64,512]{1,0:T(8,128)(2,1)} %points_hbm.1, f32[16,512]{1,0:T(8,128)} %residual_hbm.1, f32[16,512]{1,0:T(8,128)} %direction_hbm.1), custom_call_target="tpu_custom_call" | custom-call | tf_op jit(solution)/shard_map/cg_step/pallas_call | solution.py:311
  51.7 0.0 copy-done
  51.7 1.5 %fusion = (f32[16,512]{1,0:T(8,128)}, f32[16,512]{1,0:T(8,128)}, f32[16,512]{1,0:T(8,128)}) fusion(f32[16,512]{1,0:T(8,128)S(1)} %copy-done, f32[2,16,512]{2,1,0:T(8,128)} %get-tuple-element.5, f32[16,512]{1,0:T(8,128)} %residual_hbm.1, f32[16,512]{1,0:T(8,128)} %get-tuple-element.6, f32[16,512]{1,0:T(8,128)} %param.5), kind=kLoop, calls=%fused_computation.1 | loop fusion | flops 49152 | bytes 294912 | tf_op jit(solution)/shard_map/add | solution.py:337
Async XLA Ops:
  0.6 51.1 %copy-start = (f32[16,512]{1,0:T(8,128)S(1)}, f32[16,512]{1,0:T(8,128)}, u32[]{:S(2)}) copy-start(f32[16,512]{1,0:T(8,128)} %direction_hbm.1) | copy-start | bytes 98308

commit v5 on v4

--- a/solution.py
+++ b/solution.py
@@ -21,7 +21,7 @@
 
 
 def step_kernel(points_hbm, residual_hbm, direction_hbm, image, coefs, points, residual, direction,
-                blk, lhs, acc, kbuf, rs, stat, st1, st2,
+                blk, lhs, acc, k_even, k_odd, k_third, k_fourth, rs, stat, st1, st2,
                 in_sem, g_send, g_recv, r_send, r_recv, a_send, a_recv, b_send, b_recv):
     loads = [pltpu.make_async_copy(src, dst, in_sem.at[n]) for n, (src, dst) in enumerate(
         ((points_hbm, points), (direction_hbm, direction), (residual_hbm, residual)))]
@@ -109,25 +109,26 @@
         tail = jnp.where(row_id < 3, 1.0, jnp.where(row_id < 6, tail, 0.0)).astype(bf16)
         lhs[k] = jnp.concatenate([blk[k, R:SENT, :], tail], axis=0).T
 
-    def make(i, r, half_at):
+    def make(i, r, k_ref):
         s = jnp.dot(lhs[i], blk[r, R:ROWS, :], preferred_element_type=f32)
-        kbuf[half_at] = jnp.exp2(s * (math.log2(math.e) / 16.0)).astype(bf16)
-
-    def use_rows(i, r, half_at):
-        acc[i] += lax.dot_general(blk[r, 0:R, :], kbuf[half_at], (((1,), (1,)), ((), ())),
+        k_ref[...] = jnp.exp2(s * (math.log2(math.e) / 16.0)).astype(bf16)
+
+    def use_rows(i, r, k_ref):
+        acc[i] += lax.dot_general(blk[r, 0:R, :], k_ref[...], (((1,), (1,)), ((), ())),
                                   preferred_element_type=f32)
 
-    def use_columns(i, r, half_at):
-        acc[r] += jnp.dot(blk[i, 0:R, :], kbuf[half_at], preferred_element_type=f32)
+    def use_columns(i, r, k_ref):
+        acc[r] += jnp.dot(blk[i, 0:R, :], k_ref[...], preferred_element_type=f32)
 
     def own_block(k):
         arrive(k)
         if k in RELAYED:
             pass_on(k, RELAYED[k], beside(me, SIBLING)).start()
 
+    near = (k_even, k_odd)
     prepare(0)
-    make(0, 0, 0)
-    use_columns(0, 0, 0)
+    make(0, 0, k_even)
+    use_columns(0, 0, k_even)
 
     def tile(b, u):
         half, parity = lax.div(b, 2), lax.rem(b, 2)
@@ -178,12 +179,12 @@
 
     def work(b, b_next, us):
         for u in us:
-            make(*(tile(b, u + 1) if u < 3 else tile(b_next, 0)), (u + 1) % 2)
+            make(*(tile(b, u + 1) if u < 3 else tile(b_next, 0)), near[(u + 1) % 2])
             i, r = tile(b, u)
-            use_rows(i, r, u % 2)
-            use_columns(i, r, u % 2)
-
-    make(*tile(0, 0), 0)
+            use_rows(i, r, near[u % 2])
+            use_columns(i, r, near[u % 2])
+
+    make(*tile(0, 0), k_even)
     work(0, 0, range(3))
 
     for k in (6, 7):
@@ -192,7 +193,7 @@
 
     work(0, 1, (3,))
 
-    def body(b, carry):
+    def arrivals(b):
         @pl.when(b == 1)
         def _():
             own_block(4)
@@ -215,7 +216,7 @@
             def _():
                 arrive(8 + j)
 
-        for j, at in ((0, 4), (1, 5 + 100 * normal), (2, 7), (3, 8), (4, 11), (5, 12), (6, 14), (7, 14 + normal)):
+        for j, at in ((0, 4), (1, 5 + 100 * normal), (2, 7), (3, 8), (4, 11), (5, 12), (6, 14), (7, 14 + 100 * normal)):
             @pl.when(b == at)
             def _():
                 give_partner(j)
@@ -225,10 +226,12 @@
             for k in (4, 5, 6, 7):
                 give_own(k)
 
-        work(b, b + 1 - lax.div(b + 1, 16), range(4))
+    def body(b, carry):
+        arrivals(b)
+        work(b, b + 1, range(4))
         return carry
 
-    lax.fori_loop(1, 16 - special, body, 0)
+    lax.fori_loop(1, 15, body, 0)
 
     @pl.when(special == 1)
     def _():
@@ -237,19 +240,28 @@
 
     @pl.when(special == 0)
     def _():
+        give_partner(7)
+        spots = (k_even, k_odd, k_third, k_fourth)
+        for u in range(4):
+            if u < 3:
+                make(*tile(15, u + 1), spots[u + 1])
+            use_columns(*tile(15, u), spots[u])
         give_partner(1)
+        for u in range(4):
+            use_rows(*tile(15, u), spots[u])
 
     for k in (2, 3, 1):
         give_own(k)
 
-    total = direction[...] + acc[0]
+    res, dirn = residual[...], direction[...]
+    squares = jnp.sum(res * res, axis=1, keepdims=True)
+    total = dirn + acc[0]
     for slot in (8, 10, 11, 12, 13, 14, 15, 6, 7, 4, 5, 1, 2, 3, 9):
         give(slot, me).wait_recv()
         total += rs[slot]
     image[...] = total
 
-    res, dirn = residual[...], direction[...]
-    sums = [jnp.sum(v, axis=1, keepdims=True) for v in (res * res, dirn * total, res * total, total * total)]
+    sums = [squares] + [jnp.sum(v * total, axis=1, keepdims=True) for v in (dirn, res, total)]
     lane = lax.broadcasted_iota(jnp.int32, (8, 128), 1)
     packed = jnp.zeros((8, 128), f32)
     for n, v in enumerate(sums):
@@ -279,15 +291,13 @@
         packed += st2[m]
 
     def pick(n):
-        top = jnp.sum(jnp.where(lane == n, packed, 0.0), axis=1, keepdims=True)
-        bottom = jnp.sum(jnp.where(lane == n + 4, packed, 0.0), axis=1, keepdims=True)
-        return jnp.broadcast_to(jnp.concatenate([top, bottom], axis=0), (R, W))
+        return jnp.concatenate([packed[:, n:n + 1], packed[:, n + 4:n + 5]], axis=0)
 
     old, curvature, cross, square = (pick(n) for n in range(4))
     step = old / curvature
     new = old + step * (step * square - 2.0 * cross)
-    coefs[0] = step
-    coefs[1] = new / old
+    coefs[0] = jnp.broadcast_to(step, (R, W))
+    coefs[1] = jnp.broadcast_to(new / old, (R, W))
 
     for slot in range(1, 16):
         if slot < 8 or slot % 2:
@@ -320,7 +330,10 @@
             pltpu.VMEM((16, ROWS, W), bf16),
             pltpu.VMEM((8, W, DEPTH), bf16),
             pltpu.VMEM((16, R, W), f32),
-            pltpu.VMEM((2, W, W), bf16),
+            pltpu.VMEM((W, W), bf16),
+            pltpu.VMEM((W, W), bf16),
+            pltpu.VMEM((W, W), bf16),
+            pltpu.VMEM((W, W), bf16),
             pltpu.VMEM((16, R, W), f32),
             pltpu.VMEM((2, 8, 128), f32),
             pltpu.VMEM((8, 8, 128), f32),

time: 53.4 us -> 53.1 us (level)
  no operation moved by 1% of the time
where the time goes in v5:
time: 53.1 us; the launch traced here: 52.9 us
  Pallas kernels  50.8 us (96%)
  other arithmetic  1.48 us (3%)
  between operations  0.65 us (1%)
    pallas_call x1, Pallas kernels, on_device(): pl.pallas_call(step_kernel, out_shape=(jax.ShapeDtypeStruct((R, W), f32),...  50.8 us
    add x1, other arithmetic, on_device(): residual_next + beta * direction  1.48 us

profile of v5, /device:TPU:1, one launch (start us, length us, event | category | flops | bytes accessed | tf_op | source)
XLA Modules:
  0.0 52.9 jit_solution(4994037677759435271)
XLA Ops:
  0.6 0.0 copy-start
  0.6 50.8 %cg_step.1 = (f32[16,512]{1,0:T(8,128)}, f32[2,16,512]{2,1,0:T(8,128)}) custom-call(bf16[64,512]{1,0:T(8,128)(2,1)} %points_hbm.1, f32[16,512]{1,0:T(8,128)} %residual_hbm.1, f32[16,512]{1,0:T(8,128)} %direction_hbm.1), custom_call_target="tpu_custom_call" | custom-call | tf_op jit(solution)/shard_map/cg_step/pallas_call | solution.py:321
  51.4 0.0 copy-done
  51.4 1.5 %fusion = (f32[16,512]{1,0:T(8,128)}, f32[16,512]{1,0:T(8,128)}, f32[16,512]{1,0:T(8,128)}) fusion(f32[16,512]{1,0:T(8,128)S(1)} %copy-done, f32[2,16,512]{2,1,0:T(8,128)} %get-tuple-element.5, f32[16,512]{1,0:T(8,128)} %residual_hbm.1, f32[16,512]{1,0:T(8,128)} %get-tuple-element.6, f32[16,512]{1,0:T(8,128)} %param.5), kind=kLoop, calls=%fused_computation.1 | loop fusion | flops 49152 | bytes 294912 | tf_op jit(solution)/shard_map/add | solution.py:350
Async XLA Ops:
  0.6 50.8 %copy-start = (f32[16,512]{1,0:T(8,128)S(1)}, f32[16,512]{1,0:T(8,128)}, u32[]{:S(2)}) copy-start(f32[16,512]{1,0:T(8,128)} %direction_hbm.1) | copy-start | bytes 98308

commit v6 on v5

--- a/solution.py
+++ b/solution.py
@@ -53,7 +53,7 @@
     consumer = moved(4 - shift_y - square * turn, 4 - shift_z - square * (1 - turn))
 
     barrier = pltpu.get_barrier_semaphore()
-    greeted = [beside(me, k) for k in (SIBLING, 2, 3, 4)] + [partner, consumer]
+    greeted = [partner, consumer] + [beside(me, k) for k in (4, 2, 3, SIBLING)]
     for dev in greeted:
         pl.semaphore_signal(barrier, inc=1, device_id=dev, device_id_type=MESH)
 

time: 53.1 us -> 53.1 us (level)
  no operation moved by 1% of the time
where the time goes in v6:
time: 53.1 us; the launch traced here: 52.9 us
  Pallas kernels  50.8 us (96%)
  other arithmetic  1.48 us (3%)
  between operations  0.65 us (1%)
    pallas_call x1, Pallas kernels, on_device(): pl.pallas_call(step_kernel, out_shape=(jax.ShapeDtypeStruct((R, W), f32),...  50.8 us
    add x1, other arithmetic, on_device(): residual_next + beta * direction  1.48 us

profile of v6, /device:TPU:1, one launch (start us, length us, event | category | flops | bytes accessed | tf_op | source)
XLA Modules:
  0.0 52.9 jit_solution(11938276469278874566)
XLA Ops:
  0.6 0.0 copy-start
  0.6 50.8 %cg_step.1 = (f32[16,512]{1,0:T(8,128)}, f32[2,16,512]{2,1,0:T(8,128)}) custom-call(bf16[64,512]{1,0:T(8,128)(2,1)} %points_hbm.1, f32[16,512]{1,0:T(8,128)} %residual_hbm.1, f32[16,512]{1,0:T(8,128)} %direction_hbm.1), custom_call_target="tpu_custom_call" | custom-call | tf_op jit(solution)/shard_map/cg_step/pallas_call | solution.py:321
  51.4 0.0 copy-done
  51.4 1.5 %fusion = (f32[16,512]{1,0:T(8,128)}, f32[16,512]{1,0:T(8,128)}, f32[16,512]{1,0:T(8,128)}) fusion(f32[16,512]{1,0:T(8,128)S(1)} %copy-done, f32[2,16,512]{2,1,0:T(8,128)} %get-tuple-element.5, f32[16,512]{1,0:T(8,128)} %residual_hbm.1, f32[16,512]{1,0:T(8,128)} %get-tuple-element.6, f32[16,512]{1,0:T(8,128)} %param.5), kind=kLoop, calls=%fused_computation.1 | loop fusion | flops 49152 | bytes 294912 | tf_op jit(solution)/shard_map/add | solution.py:350
Async XLA Ops:
  0.6 50.8 %copy-start = (f32[16,512]{1,0:T(8,128)S(1)}, f32[16,512]{1,0:T(8,128)}, u32[]{:S(2)}) copy-start(f32[16,512]{1,0:T(8,128)} %direction_hbm.1) | copy-start | bytes 98308
